TPU v7x, 768 devices: a whole 4x8x12 slice. The times are simulated.
768 devices in a mesh: cells: 192 (over y_lo, x, z), bands: 4 (over y_hi, core).
Axes of the slice: x: 4, y: 8 (y_hi: 2, y_lo: 4; y = y_hi * 4 + y_lo), z: 12, core: 2. Of those that a mesh axis runs over, the one named last changes fastest.
Arguments:
- wavefunctions: bfloat16 [139968, 512], P('cells', 'bands'), may hold values from -6 to 6
- hamiltonians: bfloat16 [192, 729, 729], P('cells'), may hold values from -0.21875 to 0.21875
- connectivity: int32 [192, 729], P('cells'), may hold values from 0 to 728, as said below
- face_nodes: int32 [384, 81], P('cells'), may hold values from 0 to 728, as said below
Outputs:
- filtered: float32 [139968, 512], P('cells', 'bands')
- correlation: float32 [512, 512], P(None, 'bands')
Inputs may be any that keep to these rules, and one draw needn't show every extreme that they name: `connectivity`: within each partition the values are a permutation of the local node numbers laid on a lattice: cell c's node (i, j, k), 0 <= i, j, k <= 8, is lattice point (8 c + i, j, k) of the partition, so consecutive cells of a partition share 81 nodes and every local node belongs to some cell. `face_nodes`: row 0 of a partition lists the local numbers of its lattice points with first coordinate 0, row 1 those with first coordinate 8, in the order of the other two coordinates; neighbouring partitions list the same physical face nodes in the same order.
All inputs are finite; a program needn't handle non-finite values.
Results may differ from a plain program's by a relative error of at most 0.0039.
Values may be sent and summed in bfloat16 or wider, within the bound.
A program may use at most 32 MiB of HBM per device.

v0:
```python
import jax
import jax.numpy as jnp
from jax import lax
from jax.sharding import PartitionSpec as P

NODES_DEV = 729


def with_halo(cells, sides, width):
    for axis, dim in sides:
        count = lax.axis_size(axis)
        ends = count - 1
        head = lax.slice_in_dim(cells, 0, width, axis=dim)
        tail = lax.slice_in_dim(cells, cells.shape[dim] - width, cells.shape[dim], axis=dim)
        cells = jnp.concatenate(
            [
                lax.ppermute(tail, axis, [(i, (i + 1) % count) for i in range(ends)]),
                cells,
                lax.ppermute(head, axis, [((i + 1) % count, i) for i in range(ends)]),
            ],
            axis=dim,
        )
    return cells


def body(wavefunctions, hamiltonians, connectivity, face_nodes):
    node_count = wavefunctions.shape[0]
    band_width = wavefunctions.shape[1]

    def operate(vector):
        cell_rows = vector.astype(jnp.bfloat16)[connectivity]
        cell_terms = jnp.einsum(
            "cij,cjb->cib", hamiltonians, cell_rows, preferred_element_type=jnp.float32
        )
        assembled = jnp.zeros((node_count, band_width), jnp.float32)
        assembled = assembled.at[connectivity.reshape(-1)].add(cell_terms.reshape(-1, band_width))
        face_rows = assembled[face_nodes]
        face_halo = with_halo(face_rows, (("cells", 0),), 1)
        return assembled.at[face_nodes[0]].add(face_halo[0]).at[face_nodes[1]].add(face_halo[3])

    older = wavefunctions.astype(jnp.float32)
    newer = 0.5 * operate(older)
    following = operate(newer) - older
    first_part = lax.axis_index("cells") == 0
    keep_value = jnp.where(first_part, jnp.float32(1.0), jnp.float32(0.0))
    keep_rows = jnp.ones((node_count,), jnp.float32).at[face_nodes[0]].set(keep_value)
    masked = following * keep_rows[:, None]
    high_word = masked.astype(jnp.bfloat16)
    partial_gram = jnp.dot(
        lax.all_gather(high_word, "bands", axis=1, tiled=True).T,
        high_word,
        preferred_element_type=jnp.float32,
    )
    gram = lax.psum(partial_gram, "cells")
    correlation = gram / (lax.axis_size("cells") * NODES_DEV)
    return (following, correlation)


def solution(mesh):
    placed = (P("cells", "bands"), P("cells", None, None), P("cells", None), P("cells", None))
    return jax.shard_map(
        body,
        mesh=mesh,
        in_specs=placed,
        out_specs=(P("cells", "bands"), P(None, "bands")),
        check_vma=False,
    )
```

profile of v0, /device:TPU:64, one launch (start us, length us, event | category | flops | bytes accessed | tf_op | source)
XLA Modules:
  0.0 1950.0 jit_solution(13509796111675117632)
XLA Ops:
  7.2 0.0 copy-start
  7.2 0.0 all-reduce.2.cloned.1.call-start
  7.2 0.8 fusion.14
  8.0 0.7 fusion.15
  8.7 0.7 compare_select_fusion.2
  9.4 0.1 reshape.123
  9.5 2.7 gather_fusion
  12.2 0.0 copy-done
  12.2 0.0 copy-start.2
  12.2 0.5 convolution_bitcast_fusion.1
  12.7 6.1 scatter_custom_fusion
  18.8 0.7 gather_fusion.1
  19.5 10.5 collective-permute-start.1
  30.1 1.9 collective-permute-start
  32.0 0.0 copy-done.2
  32.0 4.0 collective-permute-done
  36.0 1.1 scatter_custom_fusion.1
  37.1 0.0 collective-permute-done.1
  37.1 1.1 scatter_custom_fusion.2
  38.3 2.0 gather_fusion.2
  40.4 0.5 convolution_bitcast_fusion
  40.8 0.0 copy-start.1
  40.9 6.1 scatter_custom_fusion.3
  47.0 0.7 gather_fusion.3
  47.7 1.9 collective-permute-start.2
  49.6 3.9 collective-permute-start.3
  53.5 0.8 scatter_custom_fusion.6
  54.4 0.0 collective-permute-done.2
  54.4 1.1 scatter_custom_fusion.4
  55.5 0.0 collective-permute-done.3
  55.5 1.1 scatter_custom_fusion.5
  56.7 0.0 copy-done.1
  56.7 0.8 multiply_convert_fusion
  57.5 11.1 all_gather.3
  68.6 1.1 fusion.20
  69.7 0.0 all-reduce.2.cloned.1.call-update
  69.7 1871.8 %all-reduce.2.cloned.1.call-done = f32[512,128]{1,0:T(8,128)} async-done(((f32[512,128]{1,0:T(8,128)}), f32[512,128]{1,0:T(8,128)}) %all-reduce.2.cloned.1.call-update) | async-done | bytes 262160 | tf_op jit(solution)/shard_map/psum | solution.py:54
  1941.5 1.7 broadcast_multiply_fusion
  (7 shorter events, 0.1 us)
Async XLA Ops:
  7.2 5.1 copy-start
  7.2 1934.3 %all-reduce.2.cloned.1.call-start = ((), (), s32[]{:S(2)}) async-start(), calls=%async_computation | async-start | bytes 524288 | tf_op jit(solution)/shard_map/psum | solution.py:54
  12.2 19.8 %copy-start.2 = (s32[2,81]{1,0:T(2,128)S(1)}, s32[2,81]{1,0:T(2,128)}, u32[]{:S(2)}) copy-start(s32[2,81]{1,0:T(2,128)} %param.7) | copy-start | bytes 1948
  19.5 17.6 collective-permute-start.1
  30.1 5.9 collective-permute-start
  40.8 15.8 copy-start.1
  47.7 6.7 collective-permute-start.2
  49.6 5.9 collective-permute-start.3
Sparse Core Ops, SparseCore 0:
  69.8 1871.6 all-reduce.1
where the time goes:
time: 1950 us
  waiting for transfers between devices  1880 us (96%)
  other arithmetic  21.4 us (1%)
    psum x1, waiting for transfers between devices, body(): gram = lax.psum(partial_gram, 'cells')  1870 us
  transfers between devices with their start and end apart: 5, of which 2 were waited for; matrix products, arithmetic and copies ran while one was open for 0% of the time, Pallas kernels for 0%

commit v1 on v0

v1 whole, which is shorter than its diff:
```python
import jax
import jax.numpy as jnp
from jax import lax
from jax.experimental import pallas as pl
from jax.experimental.pallas import tpu as pltpu
from jax.sharding import PartitionSpec as P

MESH = pl.DeviceIdType.MESH
NODES = 729
SHARED = 81
FAR = NODES - SHARED
WIDTH = 128
EARLY = 640
ROWS = 736
F32 = jnp.float32
BF16 = jnp.bfloat16


def mm(a, b):
    return jnp.dot(a, b, preferred_element_type=F32)


def kernel(
    sizes,
    v_hbm, h_hbm, conn_hbm,
    out_hbm, corr_ref,
    v, h, conn, u, t, y1, filt, fall, face_out, face_in,
    gram_f, gram_b, rx, ry_out, ry, rz, res,
    in_sem, out_sem, face_send, face_recv, f_send, f_recv, w_send, w_recv,
    x_send, x_recv, y_send, y_recv, z_send, z_recv, ay_send, ay_recv, ax_send, ax_recv,
):
    ny, nx, nz = sizes
    cells = lax.axis_index("cells")
    band = lax.axis_index("bands")
    last = ny * nx * nz - 1
    z = lax.rem(cells, nz)
    x = lax.rem(cells // nz, nx)
    y = cells // (nx * nz)
    core = lax.rem(band, 2)
    ring = 2 * ny
    half = ny // 2
    here = (band // 2) * ny + y

    def at(yy, xx, zz):
        return (yy * nx + xx) * nz + zz

    def f_peer(offset):
        there = lax.rem(here + offset + ring, ring)
        return (at(lax.rem(there, ny), x, z), (there // ny) * 2 + core)

    f_peers = [f_peer(half), f_peer(-half)]
    twin = (cells, band + 1 - 2 * core)
    x_peers = [(at(y, lax.rem(x + k, nx), z), band) for k in range(1, nx)]
    y_peers = [(at(lax.rem(y + k, ny), x, z), band) for k in range(1, ny)]
    z_peers = [(at(y, x, lax.rem(z + k, nz)), band) for k in range(1, nz)]

    loads = [
        pltpu.make_async_copy(conn_hbm, conn, in_sem.at[0]),
        pltpu.make_async_copy(v_hbm, v, in_sem.at[1]),
        pltpu.make_async_copy(h_hbm.at[0], h, in_sem.at[2]),
    ]
    for load in loads:
        load.start()

    barrier = pltpu.get_barrier_semaphore()
    peers = f_peers + [twin] + x_peers + y_peers + z_peers
    for peer in peers:
        pl.semaphore_signal(barrier, inc=1, device_id=peer, device_id_type=MESH)

    @pl.when(cells > 0)
    def _():
        pl.semaphore_signal(barrier, inc=1, device_id=(cells - 1, band), device_id_type=MESH)

    @pl.when(cells < last)
    def _():
        pl.semaphore_signal(barrier, inc=1, device_id=(cells + 1, band), device_id_type=MESH)

    def face_copy(step, side):
        peer = (cells - 1 + 2 * side, band)
        return pltpu.make_async_remote_copy(
            face_out.at[step, side], face_in.at[step, 1 - side],
            face_send.at[step, side], face_recv.at[step, 1 - side],
            device_id=peer, device_id_type=MESH,
        )

    def send_faces(step):
        @pl.when(cells > 0)
        def _():
            face_copy(step, 0).start()

        @pl.when(cells < last)
        def _():
            face_copy(step, 1).start()

    def wait_faces(step):
        @pl.when(cells > 0)
        def _():
            face_copy(step, 1).wait_recv()

        @pl.when(cells < last)
        def _():
            face_copy(step, 0).wait_recv()

    def done_faces(step):
        @pl.when(cells > 0)
        def _():
            face_copy(step, 0).wait_send()

        @pl.when(cells < last)
        def _():
            face_copy(step, 1).wait_send()

    @pl.when(cells == 0)
    def _():
        for step in range(2):
            face_in[step, 0] = jnp.zeros(face_in.shape[2:], BF16)

    @pl.when(cells == last)
    def _():
        for step in range(2):
            face_in[step, 1] = jnp.zeros(face_in.shape[2:], BF16)

    loads[0].wait()
    order = conn[...].astype(F32)
    column = jnp.broadcast_to(order, (WIDTH, NODES)).T
    lanes = lax.broadcasted_iota(jnp.int32, (NODES, WIDTH), 1).astype(F32)
    loads[1].wait()
    total = jnp.zeros((NODES, WIDTH), F32)
    for k in range(0, NODES, WIDTH):
        width = min(WIDTH, NODES - k)
        pick = jnp.where(column == lanes + float(k), 1.0, 0.0).astype(BF16)
        total += mm(pick[:, :width], v[k:k + width, :])
    u[0:NODES, :] = total.astype(BF16)

    loads[2].wait()
    t[0:96, :] = mm(h[0:96, :], u[0:NODES, :])
    t[EARLY:NODES, :] = mm(h[EARLY:NODES, :], u[0:NODES, :])
    face_out[0, 0, 0:SHARED, :] = t[0:SHARED, :].astype(BF16)
    face_out[0, 1, 0:SHARED, :] = t[FAR:NODES, :].astype(BF16)
    want = len(peers) + jnp.where(cells > 0, 1, 0) + jnp.where(cells < last, 1, 0)
    pl.semaphore_wait(barrier, want)
    send_faces(0)
    t[96:EARLY, :] = mm(h[96:EARLY, :], u[0:NODES, :])
    y1[0:NODES, :] = (0.5 * t[0:NODES, :]).astype(BF16)
    y1[0:SHARED, :] = jnp.zeros((SHARED, WIDTH), BF16)
    y1[FAR:NODES, :] = jnp.zeros((SHARED, WIDTH), BF16)
    low = t[0:SHARED, :]
    high = t[FAR:NODES, :]
    t[0:NODES, :] = mm(h[...], y1[0:NODES, :])

    wait_faces(0)
    low1 = 0.5 * (low + face_in[0, 0, 0:SHARED, :].astype(F32))
    high1 = 0.5 * (high + face_in[0, 1, 0:SHARED, :].astype(F32))
    y1[0:WIDTH, :] = jnp.zeros((WIDTH, WIDTH), BF16)
    y1[EARLY:NODES, :] = jnp.zeros((NODES - EARLY, WIDTH), BF16)
    y1[0:SHARED, :] = low1.astype(BF16)
    y1[FAR:NODES, :] = high1.astype(BF16)

    def add_faces(lo, hi):
        t[lo:hi, :] += mm(h[lo:hi, 0:WIDTH], y1[0:WIDTH, :]) + mm(h[lo:hi, EARLY:NODES], y1[EARLY:NODES, :])

    add_faces(0, 96)
    add_faces(EARLY, NODES)
    face_out[1, 0, 0:SHARED, :] = t[0:SHARED, :].astype(BF16)
    face_out[1, 1, 0:SHARED, :] = t[FAR:NODES, :].astype(BF16)
    send_faces(1)
    add_faces(96, EARLY)

    first = jnp.where(cells == 0, jnp.float32(1.0), jnp.float32(0.0))
    t[0:NODES, :] = t[0:NODES, :] - u[0:NODES, :].astype(F32)
    filt[0:NODES, :] = t[0:NODES, :].astype(BF16)
    filt[0:SHARED, :] = (t[0:SHARED, :] * first).astype(BF16)

    def f_copy(part, k):
        rows = pl.ds(0, EARLY) if part == 0 else pl.ds(EARLY, ROWS - EARLY)
        return pltpu.make_async_remote_copy(
            filt.at[rows], fall.at[band, rows],
            f_send.at[part, k], f_recv.at[part, k],
            device_id=f_peers[k], device_id_type=MESH,
        )

    for k in range(2):
        f_copy(0, k).start()

    wait_faces(1)
    t[0:SHARED, :] += face_in[1, 0, 0:SHARED, :].astype(F32)
    t[FAR:NODES, :] += face_in[1, 1, 0:SHARED, :].astype(F32)
    filt[EARLY:NODES, :] = t[EARLY:NODES, :].astype(BF16)
    filt[NODES:ROWS, :] = jnp.zeros((ROWS - NODES, WIDTH), BF16)
    for k in range(2):
        f_copy(1, k).start()

    rows = lax.broadcasted_iota(jnp.int32, (NODES, NODES), 0).astype(F32)
    place = jnp.where(rows == jnp.broadcast_to(order, (NODES, NODES)), 1.0, 0.0).astype(BF16)
    full = t[0:NODES, :]
    coarse = full.astype(BF16)
    fine = (full - coarse.astype(F32)).astype(BF16)
    t[0:NODES, :] = mm(place, coarse) + mm(place, fine)
    store = pltpu.make_async_copy(t.at[pl.ds(0, NODES)], out_hbm, out_sem)
    store.start()

    def w_copy(part, k):
        rows = pl.ds(0, EARLY) if part == 0 else pl.ds(EARLY, ROWS - EARLY)
        slot = (lax.rem(here - half * (1 - 2 * k) + ring, ring) // ny) * 2 + core
        return pltpu.make_async_remote_copy(
            fall.at[slot, rows], fall.at[slot, rows],
            w_send.at[part, k], w_recv.at[part, k],
            device_id=twin, device_id_type=MESH,
        )

    for part in range(2):
        for k in range(2):
            f_copy(part, k).wait_recv()
            w_copy(part, k).start()
    for part in range(2):
        for k in range(2):
            w_copy(part, k).wait_recv()

    mine = fall[band]
    for j in range(4):
        block = lax.dot_general(mine, fall[j], (((0,), (0,)), ((), ())), preferred_element_type=F32)
        gram_f[j] = block
        gram_b[j] = block.astype(BF16)

    x_copies = []
    for k in range(1, nx):
        copy = pltpu.make_async_remote_copy(
            gram_b.at[lax.rem(x + k, nx)], rx.at[k - 1],
            x_send.at[k - 1], x_recv.at[k - 1],
            device_id=x_peers[k - 1], device_id_type=MESH,
        )
        copy.start()
        x_copies.append(copy)
    part_sum = gram_f[x]
    for k in range(1, nx):
        x_copies[k - 1].wait_recv()
        part_sum += rx[k - 1].astype(F32)

    piece = WIDTH // ny
    gram_f[0] = part_sum
    ry_out[...] = part_sum.astype(BF16)
    y_copies = []
    for k in range(1, ny):
        copy = pltpu.make_async_remote_copy(
            ry_out.at[pl.ds(pl.multiple_of(lax.rem(y + k, ny) * piece, piece), piece)], ry.at[k - 1],
            y_send.at[k - 1], y_recv.at[k - 1],
            device_id=y_peers[k - 1], device_id_type=MESH,
        )
        copy.start()
        y_copies.append(copy)
    my_rows = pl.ds(pl.multiple_of(y * piece, piece), piece)
    shard = gram_f[0, my_rows, :]
    for k in range(1, ny):
        y_copies[k - 1].wait_recv()
        shard += ry[k - 1].astype(F32)

    rz[z] = shard.astype(BF16)
    z_copies = []
    for k in range(1, nz):
        copy = pltpu.make_async_remote_copy(
            rz.at[z], rz.at[z],
            z_send.at[k - 1], z_recv.at[k - 1],
            device_id=z_peers[k - 1], device_id_type=MESH,
        )
        copy.start()
        z_copies.append(copy)
    for copy in z_copies:
        copy.wait_recv()
    summed = rz[0].astype(F32)
    for k in range(1, nz):
        summed += rz[k].astype(F32)
    res[x, my_rows, :] = (summed / float((last + 1) * NODES)).astype(BF16)

    ay_copies = []
    for k in range(1, ny):
        copy = pltpu.make_async_remote_copy(
            res.at[x, my_rows], res.at[x, my_rows],
            ay_send.at[k - 1], ay_recv.at[k - 1],
            device_id=y_peers[k - 1], device_id_type=MESH,
        )
        copy.start()
        ay_copies.append(copy)
    for copy in ay_copies:
        copy.wait_recv()
    ax_copies = []
    for k in range(1, nx):
        copy = pltpu.make_async_remote_copy(
            res.at[x], res.at[x],
            ax_send.at[k - 1], ax_recv.at[k - 1],
            device_id=x_peers[k - 1], device_id_type=MESH,
        )
        copy.start()
        ax_copies.append(copy)
    for copy in ax_copies:
        copy.wait_recv()
    for j in range(4):
        corr_ref[j * WIDTH:(j + 1) * WIDTH, :] = res[j].astype(F32).T

    done_faces(0)
    done_faces(1)
    for part in range(2):
        for k in range(2):
            f_copy(part, k).wait_send()
            w_copy(part, k).wait_send()
    for copy in x_copies + y_copies + z_copies + ay_copies + ax_copies:
        copy.wait_send()
    store.wait()


def solution(mesh, sizes=(4, 4, 12)):
    ny, nx, nz = sizes
    dma = pltpu.SemaphoreType.DMA

    def body(wavefunctions, hamiltonians, connectivity, face_nodes):
        return pl.pallas_call(
            lambda *refs: kernel(sizes, *refs),
            out_shape=(
                jax.ShapeDtypeStruct((NODES, WIDTH), F32),
                jax.ShapeDtypeStruct((4 * WIDTH, WIDTH), F32),
            ),
            in_specs=[pl.BlockSpec(memory_space=pl.ANY)] * 3,
            out_specs=(
                pl.BlockSpec(memory_space=pl.ANY),
                pl.BlockSpec(memory_space=pltpu.VMEM),
            ),
            scratch_shapes=[
                pltpu.VMEM((NODES, WIDTH), BF16),
                pltpu.VMEM((NODES, NODES), BF16),
                pltpu.VMEM((1, NODES), jnp.int32),
                pltpu.VMEM((ROWS, WIDTH), BF16),
                pltpu.VMEM((ROWS, WIDTH), F32),
                pltpu.VMEM((ROWS, WIDTH), BF16),
                pltpu.VMEM((ROWS, WIDTH), BF16),
                pltpu.VMEM((4, ROWS, WIDTH), BF16),
                pltpu.VMEM((2, 2, 96, WIDTH), BF16),
                pltpu.VMEM((2, 2, 96, WIDTH), BF16),
                pltpu.VMEM((4, WIDTH, WIDTH), F32),
                pltpu.VMEM((4, WIDTH, WIDTH), BF16),
                pltpu.VMEM((nx - 1, WIDTH, WIDTH), BF16),
                pltpu.VMEM((WIDTH, WIDTH), BF16),
                pltpu.VMEM((ny - 1, WIDTH // ny, WIDTH), BF16),
                pltpu.VMEM((nz, WIDTH // ny, WIDTH), BF16),
                pltpu.VMEM((4, WIDTH, WIDTH), BF16),
                dma((3,)), dma,
                dma((2, 2)), dma((2, 2)),
                dma((2, 2)), dma((2, 2)), dma((2, 2)), dma((2, 2)),
                dma((nx - 1,)), dma((nx - 1,)),
                dma((ny - 1,)), dma((ny - 1,)),
                dma((nz - 1,)), dma((nz - 1,)),
                dma((ny - 1,)), dma((ny - 1,)),
                dma((nx - 1,)), dma((nx - 1,)),
            ],
            compiler_params=pltpu.CompilerParams(
                collective_id=0, has_side_effects=True, vmem_limit_bytes=40 << 20
            ),
        )(wavefunctions, hamiltonians, connectivity)

    return jax.shard_map(
        body,
        mesh=mesh,
        in_specs=(P("cells", "bands"), P("cells", None, None), P("cells", None), P("cells", None)),
        out_specs=(P("cells", "bands"), P(None, "bands")),
        check_vma=False,
    )
```

time: 1950 us -> 60.9 us (0.03)
  the two profiles are of different devices: /device:TPU:64 before, /device:TPU:8 now
where the time goes in v1:
time: 60.9 us; the launch traced here: 60.7 us
  Pallas kernels  55.8 us (92%)
  local copies, waits for them, and re-layouts  4.3 us (7%)
  between operations  0.65 us (1%)
    pallas_call x1, Pallas kernels, body(): pl.pallas_call(lambda *refs: kernel(sizes, *refs), out_shape=(jax.ShapeDt...  55.8 us
    unnamed x8, local copies, waits for them, and re-layouts  4.3 us

profile of v1, /device:TPU:8, one launch (start us, length us, event | category | flops | bytes accessed | tf_op | source)
XLA Modules:
  0.0 60.7 jit_solution(5480447462879319148)
XLA Ops:
  0.6 0.0 copy-start
  0.6 1.2 %copy-done = bf16[1,729,729]{2,1,0:T(8,128)(2,1)S(1)} copy-done((bf16[1,729,729]{2,1,0:T(8,128)(2,1)S(1)}, bf16[1,729,729]{2,1,0:T(8,128)(2,1)}, u32[]{:S(2)}) %copy-start) | copy-done | bytes 1062906
  1.9 0.0 copy-start.1
  1.9 0.9 %copy-done.1 = bf16[729,128]{1,0:T(8,128)(2,1)S(1)} copy-done((bf16[729,128]{1,0:T(8,128)(2,1)S(1)}, bf16[729,128]{1,0:T(8,128)(2,1)}, u32[]{:S(2)}) %copy-start.1) | copy-done | bytes 186648
  2.8 0.0 copy-start.2
  2.8 0.7 %copy-done.2 = s32[1,729]{1,0:T(1,128)S(1)} copy-done((s32[1,729]{1,0:T(1,128)S(1)}, s32[1,729]{1,0:T(1,128)}, u32[]{:S(2)}) %copy-start.2) | copy-done | bytes 2940
  3.5 55.8 %shard_map.50 = (f32[729,128]{1,0:T(8,128)S(1)}, f32[512,128]{1,0:T(8,128)S(1)}) custom-call(bf16[729,128]{1,0:T(8,128)(2,1)S(1)} %copy-done.1, bf16[1,729,729]{2,1,0:T(8,128)(2,1)S(1)} %copy-done, s32[1,729]{1,0:T(1,128)S(1)} %copy-done.2), custom_call_target="tpu_custom_call" | custom-call | tf_op jit(solution)/shard_map/pallas_call | solution.py:315
  59.3 0.7 %copy.7 = f32[729,128]{1,0:T(8,128)} copy(f32[729,128]{1,0:T(8,128)S(1)} %get-tuple-element.4) | data formatting | bytes 746496
  60.0 0.7 %copy.8 = f32[512,128]{1,0:T(8,128)} copy(f32[512,128]{1,0:T(8,128)S(1)} %get-tuple-element.5) | data formatting | bytes 524288
Async XLA Ops:
  0.6 1.3 %copy-start = (bf16[1,729,729]{2,1,0:T(8,128)(2,1)S(1)}, bf16[1,729,729]{2,1,0:T(8,128)(2,1)}, u32[]{:S(2)}) copy-start(bf16[1,729,729]{2,1,0:T(8,128)(2,1)} %refs_1_.1) | copy-start | bytes 3188650
  1.9 0.9 %copy-start.1 = (bf16[729,128]{1,0:T(8,128)(2,1)S(1)}, bf16[729,128]{1,0:T(8,128)(2,1)}, u32[]{:S(2)}) copy-start(bf16[729,128]{1,0:T(8,128)(2,1)} %refs_0_.1) | copy-start | bytes 559876
  2.8 0.7 %copy-start.2 = (s32[1,729]{1,0:T(1,128)S(1)}, s32[1,729]{1,0:T(1,128)}, u32[]{:S(2)}) copy-start(s32[1,729]{1,0:T(1,128)} %refs_2_.1) | copy-start | bytes 8752

commit v2 on v1

--- a/solution.py
+++ b/solution.py
@@ -23,10 +23,10 @@
 def kernel(
     sizes,
     v_hbm, h_hbm, conn_hbm,
-    out_hbm, corr_ref,
+    out_ref, res,
     v, h, conn, u, t, y1, filt, fall, face_out, face_in,
-    gram_f, gram_b, rx, ry_out, ry, rz, res,
-    in_sem, out_sem, face_send, face_recv, f_send, f_recv, w_send, w_recv,
+    gram_f, gram_b, rx, ry_out, ry, rz,
+    in_sem, face_send, face_recv, near, f_send, f_recv, w_send, w_recv,
     x_send, x_recv, y_send, y_recv, z_send, z_recv, ay_send, ay_recv, ax_send, ax_recv,
 ):
     ny, nx, nz = sizes
@@ -63,7 +63,23 @@
         load.start()
 
     barrier = pltpu.get_barrier_semaphore()
-    peers = f_peers + [twin] + x_peers + y_peers + z_peers
+
+    def z_peer(offset):
+        return (at(y, x, lax.rem(z + offset + nz, nz)), band)
+
+    peers = f_peers + [twin] + x_peers + y_peers + [z_peer(1), z_peer(-1)]
+
+    def meet(stage):
+        reach = (1, 2, 2)[stage]
+        for side in range(2):
+            pl.semaphore_signal(
+                near.at[stage, side], inc=1, device_id=z_peer(reach * (1 - 2 * side)), device_id_type=MESH
+            )
+
+    def met(stage):
+        for side in range(2):
+            pl.semaphore_wait(near.at[stage, side], 1)
+
     for peer in peers:
         pl.semaphore_signal(barrier, inc=1, device_id=peer, device_id_type=MESH)
 
@@ -139,6 +155,7 @@
     face_out[0, 1, 0:SHARED, :] = t[FAR:NODES, :].astype(BF16)
     want = len(peers) + jnp.where(cells > 0, 1, 0) + jnp.where(cells < last, 1, 0)
     pl.semaphore_wait(barrier, want)
+    meet(0)
     send_faces(0)
     t[96:EARLY, :] = mm(h[96:EARLY, :], u[0:NODES, :])
     y1[0:NODES, :] = (0.5 * t[0:NODES, :]).astype(BF16)
@@ -149,6 +166,8 @@
     t[0:NODES, :] = mm(h[...], y1[0:NODES, :])
 
     wait_faces(0)
+    met(0)
+    meet(1)
     low1 = 0.5 * (low + face_in[0, 0, 0:SHARED, :].astype(F32))
     high1 = 0.5 * (high + face_in[0, 1, 0:SHARED, :].astype(F32))
     y1[0:WIDTH, :] = jnp.zeros((WIDTH, WIDTH), BF16)
@@ -190,14 +209,15 @@
     for k in range(2):
         f_copy(1, k).start()
 
+    met(1)
+    meet(2)
+
     rows = lax.broadcasted_iota(jnp.int32, (NODES, NODES), 0).astype(F32)
     place = jnp.where(rows == jnp.broadcast_to(order, (NODES, NODES)), 1.0, 0.0).astype(BF16)
     full = t[0:NODES, :]
     coarse = full.astype(BF16)
     fine = (full - coarse.astype(F32)).astype(BF16)
-    t[0:NODES, :] = mm(place, coarse) + mm(place, fine)
-    store = pltpu.make_async_copy(t.at[pl.ds(0, NODES)], out_hbm, out_sem)
-    store.start()
+    out_ref[...] = mm(place, coarse) + mm(place, fine)
 
     def w_copy(part, k):
         rows = pl.ds(0, EARLY) if part == 0 else pl.ds(EARLY, ROWS - EARLY)
@@ -254,6 +274,7 @@
         y_copies[k - 1].wait_recv()
         shard += ry[k - 1].astype(F32)
 
+    met(2)
     rz[z] = shard.astype(BF16)
     z_copies = []
     for k in range(1, nz):
@@ -293,9 +314,6 @@
         ax_copies.append(copy)
     for copy in ax_copies:
         copy.wait_recv()
-    for j in range(4):
-        corr_ref[j * WIDTH:(j + 1) * WIDTH, :] = res[j].astype(F32).T
-
     done_faces(0)
     done_faces(1)
     for part in range(2):
@@ -304,7 +322,17 @@
             w_copy(part, k).wait_send()
     for copy in x_copies + y_copies + z_copies + ay_copies + ax_copies:
         copy.wait_send()
-    store.wait()
+
+
+def finish(filtered, blocks, out_hbm, corr_hbm, corr, sem):
+    first = pltpu.make_async_copy(filtered, out_hbm, sem.at[0])
+    first.start()
+    for j in range(4):
+        corr[j * WIDTH:(j + 1) * WIDTH, :] = blocks[j].astype(F32).T
+    second = pltpu.make_async_copy(corr, corr_hbm, sem.at[1])
+    second.start()
+    first.wait()
+    second.wait()
 
 
 def solution(mesh, sizes=(4, 4, 12)):
@@ -312,17 +340,14 @@
     dma = pltpu.SemaphoreType.DMA
 
     def body(wavefunctions, hamiltonians, connectivity, face_nodes):
-        return pl.pallas_call(
+        filtered, blocks = pl.pallas_call(
             lambda *refs: kernel(sizes, *refs),
             out_shape=(
                 jax.ShapeDtypeStruct((NODES, WIDTH), F32),
-                jax.ShapeDtypeStruct((4 * WIDTH, WIDTH), F32),
+                jax.ShapeDtypeStruct((4, WIDTH, WIDTH), BF16),
             ),
-            in_specs=[pl.BlockSpec(memory_space=pl.ANY)] * 3,
-            out_specs=(
-                pl.BlockSpec(memory_space=pl.ANY),
-                pl.BlockSpec(memory_space=pltpu.VMEM),
-            ),
+            in_specs=[pl.BlockSpec(memory_space=pltpu.HBM)] * 3,
+            out_specs=(pl.BlockSpec(memory_space=pltpu.VMEM),) * 2,
             scratch_shapes=[
                 pltpu.VMEM((NODES, WIDTH), BF16),
                 pltpu.VMEM((NODES, NODES), BF16),
@@ -340,9 +365,9 @@
                 pltpu.VMEM((WIDTH, WIDTH), BF16),
                 pltpu.VMEM((ny - 1, WIDTH // ny, WIDTH), BF16),
                 pltpu.VMEM((nz, WIDTH // ny, WIDTH), BF16),
-                pltpu.VMEM((4, WIDTH, WIDTH), BF16),
-                dma((3,)), dma,
+                dma((3,)),
                 dma((2, 2)), dma((2, 2)),
+                pltpu.SemaphoreType.REGULAR((3, 2)),
                 dma((2, 2)), dma((2, 2)), dma((2, 2)), dma((2, 2)),
                 dma((nx - 1,)), dma((nx - 1,)),
                 dma((ny - 1,)), dma((ny - 1,)),
@@ -353,7 +378,18 @@
             compiler_params=pltpu.CompilerParams(
                 collective_id=0, has_side_effects=True, vmem_limit_bytes=40 << 20
             ),
-        )(wavefunctions, hamiltonians, connectivity)
+        )(*[pltpu.with_memory_space_constraint(a, pltpu.HBM) for a in (wavefunctions, hamiltonians, connectivity)])
+        return pl.pallas_call(
+            finish,
+            out_shape=(
+                jax.ShapeDtypeStruct((NODES, WIDTH), F32),
+                jax.ShapeDtypeStruct((4 * WIDTH, WIDTH), F32),
+            ),
+            in_specs=[pl.BlockSpec(memory_space=pltpu.VMEM)] * 2,
+            out_specs=(pl.BlockSpec(memory_space=pltpu.HBM),) * 2,
+            scratch_shapes=[pltpu.VMEM((4 * WIDTH, WIDTH), F32), dma((2,))],
+            compiler_params=pltpu.CompilerParams(vmem_limit_bytes=16 << 20),
+        )(filtered, blocks)
 
     return jax.shard_map(
         body,

time: 60.9 us -> 54.4 us (0.89)
  the two profiles are of different devices: /device:TPU:8 before, /device:TPU:1 now
where the time goes in v2:
time: 54.4 us; the launch traced here: 53.7 us
  Pallas kernels  53 us (97%)
  between operations  0.64 us (1%)
    pallas_call x1, Pallas kernels, body(): pl.pallas_call(lambda *refs: kernel(sizes, *refs), out_shape=(jax.ShapeDt...  52.2 us

profile of v2, /device:TPU:1, one launch (start us, length us, event | category | flops | bytes accessed | tf_op | source)
XLA Modules:
  0.0 53.7 jit_solution(16216789142632025343)
XLA Ops:
  0.6 52.2 %shard_map.50 = (f32[729,128]{1,0:T(8,128)S(1)}, bf16[4,128,128]{2,1,0:T(8,128)(2,1)S(1)}) custom-call(bf16[729,128]{1,0:T(8,128)(2,1)} %refs_0_.1, bf16[1,729,729]{2,1,0:T(8,128)(2,1)} %refs_1_.1, s32[1,729]{1,0:T(1,128)} %refs_2_.1), custom_call_target="tpu_custom_call" | custom-call | tf_op jit(solution)/shard_map/pallas_call | solution.py:343
  52.8 0.8 %shard_map.51 = (f32[729,128]{1,0:T(8,128)}, f32[512,128]{1,0:T(8,128)}) custom-call(f32[729,128]{1,0:T(8,128)S(1)} %get-tuple-element.4.filtered, bf16[4,128,128]{2,1,0:T(8,128)(2,1)S(1)} %get-tuple-element.5.blocks), custom_call_target="tpu_custom_call" | custom-call | tf_op jit(solution)/shard_map/pallas_call | solution.py:382

commit v3 on v2

v3 whole, which is shorter than its diff:
```python
import jax
import jax.numpy as jnp
from jax import lax
from jax.experimental import pallas as pl
from jax.experimental.pallas import tpu as pltpu
from jax.sharding import PartitionSpec as P

MESH = pl.DeviceIdType.MESH
NODES = 729
SHARED = 81
FAR = NODES - SHARED
WIDTH = 128
EARLY = 640
ROWS = 736
F32 = jnp.float32
BF16 = jnp.bfloat16


def mm(a, b):
    return jnp.dot(a, b, preferred_element_type=F32)


def kernel(
    sizes,
    v_hbm, h_hbm, conn_hbm,
    out_ref, res,
    v, h, conn, u, t, y1, filt, fall, own_twin, far_twin, face_out, face_in,
    gram_f, gram_b, rs_in, rz,
    in_sem, face_send, face_recv, near, f_send, f_recv, w_send, w_recv,
    s_send, s_recv, z_send, z_recv, g_send, g_recv,
):
    ny, nx, nz = sizes
    cells = lax.axis_index("cells")
    band = lax.axis_index("bands")
    last = ny * nx * nz - 1
    z = lax.rem(cells, nz)
    x = lax.rem(cells // nz, nx)
    y = cells // (nx * nz)
    core = lax.rem(band, 2)
    plane = band // 2
    ring = 2 * ny
    half = ny // 2
    here = plane * ny + y

    def at(yy, xx, zz):
        return (yy * nx + xx) * nz + zz

    def f_peer(offset):
        there = lax.rem(here + offset + ring, ring)
        return (at(lax.rem(there, ny), x, z), (there // ny) * 2 + core)

    def x_peer(offset):
        return (at(y, lax.rem(x + offset + nx, nx), z), band)

    def z_peer(offset):
        return (at(y, x, lax.rem(z + offset + nz, nz)), band)

    def mirror(j):
        return (y, y + 1 - 2 * lax.rem(y, 2), lax.rem(y + 2, 4), 3 - y)[j]

    def xy_peer(i, j):
        return (at(mirror(j), lax.rem(x + i, nx), z), band)

    f_peers = [f_peer(half), f_peer(-half)]
    twin = (cells, band + 1 - 2 * core)
    spans = [(i, j) for i in range(nx) for j in range(ny) if i + j]
    spans.sort(key=lambda s: -(min(s[0], nx - s[0]) + s[1]))
    z_spans = sorted(range(1, nz), key=lambda k: -min(k, nz - k))

    loads = [
        pltpu.make_async_copy(conn_hbm, conn, in_sem.at[0]),
        pltpu.make_async_copy(v_hbm, v, in_sem.at[1]),
        pltpu.make_async_copy(h_hbm.at[0], h, in_sem.at[2]),
    ]
    for load in loads:
        load.start()

    barrier = pltpu.get_barrier_semaphore()
    peers = f_peers + [twin, xy_peer(0, 1), x_peer(1), x_peer(-1), z_peer(1), z_peer(-1)]
    meetings = (
        (xy_peer(0, 1), x_peer(1), x_peer(-1), z_peer(1), z_peer(-1)),
        (x_peer(1), x_peer(-1), x_peer(2), z_peer(2), z_peer(-2)),
        (z_peer(2), z_peer(-2)),
    )

    def meet(stage):
        for slot, peer in enumerate(meetings[stage]):
            pl.semaphore_signal(near.at[stage, slot], inc=1, device_id=peer, device_id_type=MESH)

    def met(stage):
        for slot in range(len(meetings[stage])):
            pl.semaphore_wait(near.at[stage, slot], 1)

    for peer in peers:
        pl.semaphore_signal(barrier, inc=1, device_id=peer, device_id_type=MESH)

    @pl.when(cells > 0)
    def _():
        pl.semaphore_signal(barrier, inc=1, device_id=(cells - 1, band), device_id_type=MESH)

    @pl.when(cells < last)
    def _():
        pl.semaphore_signal(barrier, inc=1, device_id=(cells + 1, band), device_id_type=MESH)

    def face_copy(step, side):
        peer = (cells - 1 + 2 * side, band)
        return pltpu.make_async_remote_copy(
            face_out.at[step, side], face_in.at[step, 1 - side],
            face_send.at[step, side], face_recv.at[step, 1 - side],
            device_id=peer, device_id_type=MESH,
        )

    def send_faces(step):
        @pl.when(cells > 0)
        def _():
            face_copy(step, 0).start()

        @pl.when(cells < last)
        def _():
            face_copy(step, 1).start()

    def wait_faces(step):
        @pl.when(cells > 0)
        def _():
            face_copy(step, 1).wait_recv()

        @pl.when(cells < last)
        def _():
            face_copy(step, 0).wait_recv()

    def done_faces(step):
        @pl.when(cells > 0)
        def _():
            face_copy(step, 0).wait_send()

        @pl.when(cells < last)
        def _():
            face_copy(step, 1).wait_send()

    @pl.when(cells == 0)
    def _():
        for step in range(2):
            face_in[step, 0] = jnp.zeros(face_in.shape[2:], BF16)

    @pl.when(cells == last)
    def _():
        for step in range(2):
            face_in[step, 1] = jnp.zeros(face_in.shape[2:], BF16)

    loads[0].wait()
    order = conn[...].astype(F32)
    column = jnp.broadcast_to(order, (WIDTH, NODES)).T
    lanes = lax.broadcasted_iota(jnp.int32, (NODES, WIDTH), 1).astype(F32)
    loads[1].wait()
    total = jnp.zeros((NODES, WIDTH), F32)
    for k in range(0, NODES, WIDTH):
        width = min(WIDTH, NODES - k)
        pick = jnp.where(column == lanes + float(k), 1.0, 0.0).astype(BF16)
        total += mm(pick[:, :width], v[k:k + width, :])
    u[0:NODES, :] = total.astype(BF16)

    loads[2].wait()
    t[0:96, :] = mm(h[0:96, :], u[0:NODES, :])
    t[EARLY:NODES, :] = mm(h[EARLY:NODES, :], u[0:NODES, :])
    face_out[0, 0, 0:SHARED, :] = t[0:SHARED, :].astype(BF16)
    face_out[0, 1, 0:SHARED, :] = t[FAR:NODES, :].astype(BF16)
    want = len(peers) + jnp.where(cells > 0, 1, 0) + jnp.where(cells < last, 1, 0)
    pl.semaphore_wait(barrier, want)
    meet(0)
    send_faces(0)
    t[96:EARLY, :] = mm(h[96:EARLY, :], u[0:NODES, :])
    y1[0:NODES, :] = (0.5 * t[0:NODES, :]).astype(BF16)
    y1[0:SHARED, :] = jnp.zeros((SHARED, WIDTH), BF16)
    y1[FAR:NODES, :] = jnp.zeros((SHARED, WIDTH), BF16)
    low = t[0:SHARED, :]
    high = t[FAR:NODES, :]
    t[0:NODES, :] = mm(h[...], y1[0:NODES, :])

    wait_faces(0)
    met(0)
    meet(1)
    low1 = 0.5 * (low + face_in[0, 0, 0:SHARED, :].astype(F32))
    high1 = 0.5 * (high + face_in[0, 1, 0:SHARED, :].astype(F32))
    y1[0:WIDTH, :] = jnp.zeros((WIDTH, WIDTH), BF16)
    y1[EARLY:NODES, :] = jnp.zeros((NODES - EARLY, WIDTH), BF16)
    y1[0:SHARED, :] = low1.astype(BF16)
    y1[FAR:NODES, :] = high1.astype(BF16)

    def add_faces(lo, hi):
        t[lo:hi, :] += mm(h[lo:hi, 0:WIDTH], y1[0:WIDTH, :]) + mm(h[lo:hi, EARLY:NODES], y1[EARLY:NODES, :])

    add_faces(0, 96)
    add_faces(EARLY, NODES)
    face_out[1, 0, 0:SHARED, :] = t[0:SHARED, :].astype(BF16)
    face_out[1, 1, 0:SHARED, :] = t[FAR:NODES, :].astype(BF16)
    send_faces(1)
    add_faces(96, EARLY)

    first = jnp.where(cells == 0, jnp.float32(1.0), jnp.float32(0.0))
    t[0:NODES, :] = t[0:NODES, :] - u[0:NODES, :].astype(F32)
    filt[0:NODES, :] = t[0:NODES, :].astype(BF16)
    filt[0:SHARED, :] = (t[0:SHARED, :] * first).astype(BF16)

    def rows_of(part):
        return pl.ds(0, EARLY) if part == 0 else pl.ds(EARLY, ROWS - EARLY)

    def f_copy(part, k):
        return pltpu.make_async_remote_copy(
            filt.at[rows_of(part)], fall.at[plane, rows_of(part)],
            f_send.at[part, k], f_recv.at[part, k],
            device_id=f_peers[k], device_id_type=MESH,
        )

    for k in range(2):
        f_copy(0, k).start()

    wait_faces(1)
    t[FAR:NODES, :] += face_in[1, 1, 0:SHARED, :].astype(F32)
    filt[EARLY:NODES, :] = t[EARLY:NODES, :].astype(BF16)
    filt[NODES:ROWS, :] = jnp.zeros((ROWS - NODES, WIDTH), BF16)
    for k in range(2):
        f_copy(1, k).start()
    own_copy = pltpu.make_async_remote_copy(
        filt, own_twin, w_send.at[2], w_recv.at[2], device_id=twin, device_id_type=MESH
    )
    own_copy.start()
    met(1)
    meet(2)

    t[0:SHARED, :] += face_in[1, 0, 0:SHARED, :].astype(F32)
    rows = lax.broadcasted_iota(jnp.int32, (NODES, NODES), 0).astype(F32)
    place = jnp.where(rows == jnp.broadcast_to(order, (NODES, NODES)), 1.0, 0.0).astype(BF16)
    full = t[0:NODES, :]
    coarse = full.astype(BF16)
    fine = (full - coarse.astype(F32)).astype(BF16)
    out_ref[...] = mm(place, coarse) + mm(place, fine)

    def gram(part, left, one, two):
        for side, right in ((core, one), (1 - core, two)):
            block = lax.dot_general(left, right, (((0,), (0,)), ((), ())), preferred_element_type=F32)
            tiles = block.reshape(8, 16, WIDTH)
            gram_f[part, pl.ds(8 * side, 8)] = tiles
            gram_b[part, pl.ds(8 * side, 8)] = tiles.astype(BF16)

    mine = x * ny + y

    def s_copy(part, n):
        i, j = spans[n]
        shard = lax.rem(x + i, nx) * ny + mirror(j)
        return pltpu.make_async_remote_copy(
            gram_b.at[part, shard], rs_in.at[part, n],
            s_send.at[part, n], s_recv.at[part, n],
            device_id=xy_peer(i, j), device_id_type=MESH,
        )

    def z_copy(part, n):
        return pltpu.make_async_remote_copy(
            rz.at[part, z], rz.at[part, z],
            z_send.at[part, n], z_recv.at[part, n],
            device_id=z_peer(z_spans[n]), device_id_type=MESH,
        )

    def g_copy(part, n):
        i, j = spans[n]
        block = plane if part == 0 else 1 - plane
        return pltpu.make_async_remote_copy(
            res.at[block, mine], res.at[block, mine],
            g_send.at[part, n], g_recv.at[part, n],
            device_id=xy_peer(i, j), device_id_type=MESH,
        )

    def scatter(part):
        for n in range(len(spans)):
            s_copy(part, n).start()

    def exchange(part):
        total = gram_f[part, mine]
        for n in range(len(spans)):
            s_copy(part, n).wait_recv()
        for n in range(len(spans)):
            total += rs_in[part, n].astype(F32)
        rz[part, z] = total.astype(BF16)
        for n in range(len(z_spans)):
            z_copy(part, n).start()

    def spread(part):
        for n in range(len(z_spans)):
            z_copy(part, n).wait_recv()
        total = rz[part, 0].astype(F32)
        for k in range(1, nz):
            total += rz[part, k].astype(F32)
        res[plane if part == 0 else 1 - plane, mine] = (total / float((last + 1) * NODES)).astype(BF16)
        for n in range(len(spans)):
            g_copy(part, n).start()

    own_copy.wait_recv()
    gram(0, filt[...], filt[...], own_twin[...])
    scatter(0)

    def w_copy(part):
        return pltpu.make_async_remote_copy(
            fall.at[1 - plane, rows_of(part)], far_twin.at[rows_of(part)],
            w_send.at[part], w_recv.at[part],
            device_id=twin, device_id_type=MESH,
        )

    for part in range(2):
        for k in range(2):
            f_copy(part, k).wait_recv()
        w_copy(part).start()
    met(2)
    exchange(0)
    for part in range(2):
        w_copy(part).wait_recv()
    gram(1, fall[plane], fall[1 - plane], far_twin[...])
    scatter(1)
    exchange(1)
    spread(0)
    spread(1)
    for part in range(2):
        for n in range(len(spans)):
            g_copy(part, n).wait_recv()

    done_faces(0)
    done_faces(1)
    own_copy.wait_send()
    for part in range(2):
        w_copy(part).wait_send()
        for k in range(2):
            f_copy(part, k).wait_send()
        for n in range(len(spans)):
            s_copy(part, n).wait_send()
            g_copy(part, n).wait_send()
        for n in range(len(z_spans)):
            z_copy(part, n).wait_send()


def finish(filtered, blocks, out_hbm, corr_hbm, corr, sem):
    first = pltpu.make_async_copy(filtered, out_hbm, sem.at[0])
    first.start()
    for j in range(4):
        corr[j * WIDTH:(j + 1) * WIDTH, :] = blocks[j].astype(F32).T
    second = pltpu.make_async_copy(corr, corr_hbm, sem.at[1])
    second.start()
    first.wait()
    second.wait()


def solution(mesh, sizes=(4, 4, 12)):
    ny, nx, nz = sizes
    dma = pltpu.SemaphoreType.DMA

    def body(wavefunctions, hamiltonians, connectivity, face_nodes):
        filtered, blocks = pl.pallas_call(
            lambda *refs: kernel(sizes, *refs),
            out_shape=(
                jax.ShapeDtypeStruct((NODES, WIDTH), F32),
                jax.ShapeDtypeStruct((2, 16, 16, WIDTH), BF16),
            ),
            in_specs=[pl.BlockSpec(memory_space=pltpu.HBM)] * 3,
            out_specs=(pl.BlockSpec(memory_space=pltpu.VMEM),) * 2,
            scratch_shapes=[
                pltpu.VMEM((NODES, WIDTH), BF16),
                pltpu.VMEM((NODES, NODES), BF16),
                pltpu.VMEM((1, NODES), jnp.int32),
                pltpu.VMEM((ROWS, WIDTH), BF16),
                pltpu.VMEM((ROWS, WIDTH), F32),
                pltpu.VMEM((ROWS, WIDTH), BF16),
                pltpu.VMEM((ROWS, WIDTH), BF16),
                pltpu.VMEM((2, ROWS, WIDTH), BF16),
                pltpu.VMEM((ROWS, WIDTH), BF16),
                pltpu.VMEM((ROWS, WIDTH), BF16),
                pltpu.VMEM((2, 2, 96, WIDTH), BF16),
                pltpu.VMEM((2, 2, 96, WIDTH), BF16),
                pltpu.VMEM((2, 16, 16, WIDTH), F32),
                pltpu.VMEM((2, 16, 16, WIDTH), BF16),
                pltpu.VMEM((2, nx * ny - 1, 16, WIDTH), BF16),
                pltpu.VMEM((2, nz, 16, WIDTH), BF16),
                dma((3,)),
                dma((2, 2)), dma((2, 2)),
                pltpu.SemaphoreType.REGULAR((3, 5)),
                dma((2, 2)), dma((2, 2)), dma((3,)), dma((3,)),
                dma((2, nx * ny - 1)), dma((2, nx * ny - 1)),
                dma((2, nz - 1)), dma((2, nz - 1)),
                dma((2, nx * ny - 1)), dma((2, nx * ny - 1)),
            ],
            compiler_params=pltpu.CompilerParams(
                collective_id=0, has_side_effects=True, vmem_limit_bytes=40 << 20
            ),
        )(*[pltpu.with_memory_space_constraint(a, pltpu.HBM) for a in (wavefunctions, hamiltonians, connectivity)])
        return pl.pallas_call(
            finish,
            out_shape=(
                jax.ShapeDtypeStruct((NODES, WIDTH), F32),
                jax.ShapeDtypeStruct((4 * WIDTH, WIDTH), F32),
            ),
            in_specs=[pl.BlockSpec(memory_space=pltpu.VMEM)] * 2,
            out_specs=(pl.BlockSpec(memory_space=pltpu.HBM),) * 2,
            scratch_shapes=[pltpu.VMEM((4 * WIDTH, WIDTH), F32), dma((2,))],
            compiler_params=pltpu.CompilerParams(vmem_limit_bytes=16 << 20),
        )(filtered, blocks.reshape(4, WIDTH, WIDTH))

    return jax.shard_map(
        body,
        mesh=mesh,
        in_specs=(P("cells", "bands"), P("cells", None, None), P("cells", None), P("cells", None)),
        out_specs=(P("cells", "bands"), P(None, "bands")),
        check_vma=False,
    )
```

time: 54.4 us -> 50.8 us (0.934)
  Pallas kernels: 53 us -> 50 us
    pallas_call x1, Pallas kernels: 52.2 us -> 49.1 us  [body(): pl.pallas_call(lambda *refs: kernel(sizes, *refs), out_shape=(jax.ShapeDt...]
where the time goes in v3:
time: 50.8 us; the launch traced here: 50.6 us
  Pallas kernels  50 us (98%)
  between operations  0.64 us (1%)
    pallas_call x1, Pallas kernels, body(): pl.pallas_call(lambda *refs: kernel(sizes, *refs), out_shape=(jax.ShapeDt...  49.1 us

profile of v3, /device:TPU:1, one launch (start us, length us, event | category | flops | bytes accessed | tf_op | source)
XLA Modules:
  0.0 50.6 jit_solution(10410248859954165648)
XLA Ops:
  0.6 49.1 %shard_map.50 = (f32[729,128]{1,0:T(8,128)S(1)}, bf16[2,16,16,128]{3,2,1,0:T(8,128)(2,1)S(1)}) custom-call(bf16[729,128]{1,0:T(8,128)(2,1)} %refs_0_.1, bf16[1,729,729]{2,1,0:T(8,128)(2,1)} %refs_1_.1, s32[1,729]{1,0:T(1,128)} %refs_2_.1), custom_call_target="tpu_custom_call" | custom-call | tf_op jit(solution)/shard_map/pallas_call | solution.py:354
  49.8 0.8 %shard_map.51 = (f32[729,128]{1,0:T(8,128)}, f32[512,128]{1,0:T(8,128)}) custom-call(f32[729,128]{1,0:T(8,128)S(1)} %get-tuple-element.4.filtered, bf16[4,128,128]{2,1,0:T(8,128)(2,1)S(1)} %bitcast.1), custom_call_target="tpu_custom_call" | custom-call | tf_op jit(solution)/shard_map/pallas_call | solution.py:391

commit v4 on v3

--- a/solution.py
+++ b/solution.py
@@ -11,6 +11,7 @@
 FAR = NODES - SHARED
 WIDTH = 128
 EARLY = 640
+LOW = 80
 ROWS = 736
 F32 = jnp.float32
 BF16 = jnp.bfloat16
@@ -70,13 +71,18 @@
     loads = [
         pltpu.make_async_copy(conn_hbm, conn, in_sem.at[0]),
         pltpu.make_async_copy(v_hbm, v, in_sem.at[1]),
-        pltpu.make_async_copy(h_hbm.at[0], h, in_sem.at[2]),
+        pltpu.make_async_copy(h_hbm.at[0, pl.ds(0, 96)], h.at[pl.ds(0, 96)], in_sem.at[2]),
+        pltpu.make_async_copy(
+            h_hbm.at[0, pl.ds(EARLY, NODES - EARLY)], h.at[pl.ds(EARLY, NODES - EARLY)], in_sem.at[3]
+        ),
+        pltpu.make_async_copy(h_hbm.at[0, pl.ds(96, EARLY - 96)], h.at[pl.ds(96, EARLY - 96)], in_sem.at[4]),
     ]
     for load in loads:
         load.start()
 
     barrier = pltpu.get_barrier_semaphore()
-    peers = f_peers + [twin, xy_peer(0, 1), x_peer(1), x_peer(-1), z_peer(1), z_peer(-1)]
+    cross = (at(lax.rem(y + half, ny), x, z), (1 - plane) * 2 + 1 - core)
+    peers = f_peers + [cross, twin, xy_peer(0, 1), x_peer(1), x_peer(-1), z_peer(1), z_peer(-1)]
     meetings = (
         (xy_peer(0, 1), x_peer(1), x_peer(-1), z_peer(1), z_peer(-1)),
         (x_peer(1), x_peer(-1), x_peer(2), z_peer(2), z_peer(-2)),
@@ -146,6 +152,14 @@
     def _():
         for step in range(2):
             face_in[step, 1] = jnp.zeros(face_in.shape[2:], BF16)
+
+    far_first = at(lax.rem(y + half, ny), x, z) == 0
+
+    @pl.when(jnp.logical_not(far_first))
+    def _():
+        fall[0, 0:LOW, :] = jnp.zeros((LOW, WIDTH), BF16)
+        fall[1, 0:LOW, :] = jnp.zeros((LOW, WIDTH), BF16)
+        far_twin[0:LOW, :] = jnp.zeros((LOW, WIDTH), BF16)
 
     loads[0].wait()
     order = conn[...].astype(F32)
@@ -160,6 +174,7 @@
     u[0:NODES, :] = total.astype(BF16)
 
     loads[2].wait()
+    loads[3].wait()
     t[0:96, :] = mm(h[0:96, :], u[0:NODES, :])
     t[EARLY:NODES, :] = mm(h[EARLY:NODES, :], u[0:NODES, :])
     face_out[0, 0, 0:SHARED, :] = t[0:SHARED, :].astype(BF16)
@@ -168,6 +183,7 @@
     pl.semaphore_wait(barrier, want)
     meet(0)
     send_faces(0)
+    loads[4].wait()
     t[96:EARLY, :] = mm(h[96:EARLY, :], u[0:NODES, :])
     y1[0:NODES, :] = (0.5 * t[0:NODES, :]).astype(BF16)
     y1[0:SHARED, :] = jnp.zeros((SHARED, WIDTH), BF16)
@@ -202,7 +218,7 @@
     filt[0:SHARED, :] = (t[0:SHARED, :] * first).astype(BF16)
 
     def rows_of(part):
-        return pl.ds(0, EARLY) if part == 0 else pl.ds(EARLY, ROWS - EARLY)
+        return (pl.ds(LOW, EARLY - LOW), pl.ds(EARLY, ROWS - EARLY), pl.ds(0, LOW))[part]
 
     def f_copy(part, k):
         return pltpu.make_async_remote_copy(
@@ -213,6 +229,16 @@
 
     for k in range(2):
         f_copy(0, k).start()
+
+    @pl.when(cells == 0)
+    def _():
+        for k in range(2):
+            f_copy(2, k).start()
+
+    cross_copy = pltpu.make_async_remote_copy(
+        filt.at[rows_of(1)], far_twin.at[rows_of(1)],
+        w_send.at[1], w_recv.at[1], device_id=cross, device_id_type=MESH,
+    )
 
     wait_faces(1)
     t[FAR:NODES, :] += face_in[1, 1, 0:SHARED, :].astype(F32)
@@ -220,8 +246,9 @@
     filt[NODES:ROWS, :] = jnp.zeros((ROWS - NODES, WIDTH), BF16)
     for k in range(2):
         f_copy(1, k).start()
+    cross_copy.start()
     own_copy = pltpu.make_async_remote_copy(
-        filt, own_twin, w_send.at[2], w_recv.at[2], device_id=twin, device_id_type=MESH
+        filt, own_twin, w_send.at[3], w_recv.at[3], device_id=twin, device_id_type=MESH
     )
     own_copy.start()
     met(1)
@@ -249,14 +276,14 @@
         shard = lax.rem(x + i, nx) * ny + mirror(j)
         return pltpu.make_async_remote_copy(
             gram_b.at[part, shard], rs_in.at[part, n],
-            s_send.at[part, n], s_recv.at[part, n],
+            s_send.at[part], s_recv.at[part],
             device_id=xy_peer(i, j), device_id_type=MESH,
         )
 
     def z_copy(part, n):
         return pltpu.make_async_remote_copy(
             rz.at[part, z], rz.at[part, z],
-            z_send.at[part, n], z_recv.at[part, n],
+            z_send.at[part], z_recv.at[part],
             device_id=z_peer(z_spans[n]), device_id_type=MESH,
         )
 
@@ -265,9 +292,21 @@
         block = plane if part == 0 else 1 - plane
         return pltpu.make_async_remote_copy(
             res.at[block, mine], res.at[block, mine],
-            g_send.at[part, n], g_recv.at[part, n],
+            g_send.at[part], g_recv.at[part],
             device_id=xy_peer(i, j), device_id_type=MESH,
         )
+
+    def all_of(ref, send, recv):
+        return pltpu.make_async_remote_copy(ref, ref, send, recv, device_id=twin, device_id_type=MESH)
+
+    def s_all(part):
+        return all_of(rs_in.at[part], s_send.at[part], s_recv.at[part])
+
+    def z_all(part):
+        return all_of(rz.at[part, pl.ds(0, nz - 1)], z_send.at[part], z_recv.at[part])
+
+    def g_all(part):
+        return all_of(rs_in.at[part], g_send.at[part], g_recv.at[part])
 
     def scatter(part):
         for n in range(len(spans)):
@@ -275,8 +314,7 @@
 
     def exchange(part):
         total = gram_f[part, mine]
-        for n in range(len(spans)):
-            s_copy(part, n).wait_recv()
+        s_all(part).wait_recv()
         for n in range(len(spans)):
             total += rs_in[part, n].astype(F32)
         rz[part, z] = total.astype(BF16)
@@ -284,8 +322,7 @@
             z_copy(part, n).start()
 
     def spread(part):
-        for n in range(len(z_spans)):
-            z_copy(part, n).wait_recv()
+        z_all(part).wait_recv()
         total = rz[part, 0].astype(F32)
         for k in range(1, nz):
             total += rz[part, k].astype(F32)
@@ -304,35 +341,52 @@
             device_id=twin, device_id_type=MESH,
         )
 
-    for part in range(2):
+    for k in range(2):
+        f_copy(0, k).wait_recv()
+    w_copy(0).start()
+
+    @pl.when(far_first)
+    def _():
         for k in range(2):
-            f_copy(part, k).wait_recv()
-        w_copy(part).start()
+            f_copy(2, k).wait_recv()
+        w_copy(2).start()
+        w_copy(2).wait_recv()
+
+    for k in range(2):
+        f_copy(1, k).wait_recv()
+    cross_copy.wait_recv()
+    w_copy(0).wait_recv()
+    gram(1, fall[plane], fall[1 - plane], far_twin[...])
+    scatter(1)
     met(2)
     exchange(0)
-    for part in range(2):
-        w_copy(part).wait_recv()
-    gram(1, fall[plane], fall[1 - plane], far_twin[...])
-    scatter(1)
     exchange(1)
     spread(0)
     spread(1)
     for part in range(2):
-        for n in range(len(spans)):
-            g_copy(part, n).wait_recv()
+        g_all(part).wait_recv()
 
     done_faces(0)
     done_faces(1)
     own_copy.wait_send()
+    cross_copy.wait_send()
+    w_copy(0).wait_send()
+
+    @pl.when(far_first)
+    def _():
+        w_copy(2).wait_send()
+
+    @pl.when(cells == 0)
+    def _():
+        for k in range(2):
+            f_copy(2, k).wait_send()
+
     for part in range(2):
-        w_copy(part).wait_send()
         for k in range(2):
             f_copy(part, k).wait_send()
-        for n in range(len(spans)):
-            s_copy(part, n).wait_send()
-            g_copy(part, n).wait_send()
-        for n in range(len(z_spans)):
-            z_copy(part, n).wait_send()
+        s_all(part).wait_send()
+        z_all(part).wait_send()
+        g_all(part).wait_send()
 
 
 def finish(filtered, blocks, out_hbm, corr_hbm, corr, sem):
@@ -376,13 +430,11 @@
                 pltpu.VMEM((2, 16, 16, WIDTH), BF16),
                 pltpu.VMEM((2, nx * ny - 1, 16, WIDTH), BF16),
                 pltpu.VMEM((2, nz, 16, WIDTH), BF16),
-                dma((3,)),
+                dma((5,)),
                 dma((2, 2)), dma((2, 2)),
                 pltpu.SemaphoreType.REGULAR((3, 5)),
-                dma((2, 2)), dma((2, 2)), dma((3,)), dma((3,)),
-                dma((2, nx * ny - 1)), dma((2, nx * ny - 1)),
-                dma((2, nz - 1)), dma((2, nz - 1)),
-                dma((2, nx * ny - 1)), dma((2, nx * ny - 1)),
+                dma((3, 2)), dma((3, 2)), dma((4,)), dma((4,)),
+                dma((2,)), dma((2,)), dma((2,)), dma((2,)), dma((2,)), dma((2,)),
             ],
             compiler_params=pltpu.CompilerParams(
                 collective_id=0, has_side_effects=True, vmem_limit_bytes=40 << 20

time: 50.8 us -> 48.8 us (0.961)
  Pallas kernels: 50 us -> 48 us
    pallas_call x1, Pallas kernels: 49.1 us -> 47.2 us  [body(): pl.pallas_call(lambda *refs: kernel(sizes, *refs), out_shape=(jax.ShapeDt...]
where the time goes in v4:
time: 48.8 us; the launch traced here: 48.7 us
  Pallas kernels  48 us (98%)
  between operations  0.64 us (1%)
    pallas_call x1, Pallas kernels, body(): pl.pallas_call(lambda *refs: kernel(sizes, *refs), out_shape=(jax.ShapeDt...  47.2 us

profile of v4, /device:TPU:1, one launch (start us, length us, event | category | flops | bytes accessed | tf_op | source)
XLA Modules:
  0.0 48.7 jit_solution(1128673696527725453)
XLA Ops:
  0.6 47.2 %shard_map.50 = (f32[729,128]{1,0:T(8,128)S(1)}, bf16[2,16,16,128]{3,2,1,0:T(8,128)(2,1)S(1)}) custom-call(bf16[729,128]{1,0:T(8,128)(2,1)} %refs_0_.1, bf16[1,729,729]{2,1,0:T(8,128)(2,1)} %refs_1_.1, s32[1,729]{1,0:T(1,128)} %refs_2_.1), custom_call_target="tpu_custom_call" | custom-call | tf_op jit(solution)/shard_map/pallas_call | solution.py:408
  47.8 0.8 %shard_map.51 = (f32[729,128]{1,0:T(8,128)}, f32[512,128]{1,0:T(8,128)}) custom-call(f32[729,128]{1,0:T(8,128)S(1)} %get-tuple-element.4.filtered, bf16[4,128,128]{2,1,0:T(8,128)(2,1)S(1)} %bitcast.1), custom_call_target="tpu_custom_call" | custom-call | tf_op jit(solution)/shard_map/pallas_call | solution.py:443

commit v5 on v4

--- a/solution.py
+++ b/solution.py
@@ -12,6 +12,7 @@
 WIDTH = 128
 EARLY = 640
 LOW = 80
+CUT = 400
 ROWS = 736
 F32 = jnp.float32
 BF16 = jnp.bfloat16
@@ -25,9 +26,9 @@
     sizes,
     v_hbm, h_hbm, conn_hbm,
     out_ref, res,
-    v, h, conn, u, t, y1, filt, fall, own_twin, far_twin, face_out, face_in,
+    v, h, conn, u, t, y1, filt, whole, fall, own_twin, far_twin, late, face_out, face_in, next_in,
     gram_f, gram_b, rs_in, rz,
-    in_sem, face_send, face_recv, near, f_send, f_recv, w_send, w_recv,
+    in_sem, face_send, face_recv, near, link, next_send, next_recv, f_send, f_recv, w_send, w_recv,
     s_send, s_recv, z_send, z_recv, g_send, g_recv,
 ):
     ny, nx, nz = sizes
@@ -90,12 +91,11 @@
     )
 
     def meet(stage):
-        for slot, peer in enumerate(meetings[stage]):
-            pl.semaphore_signal(near.at[stage, slot], inc=1, device_id=peer, device_id_type=MESH)
+        for peer in meetings[stage]:
+            pl.semaphore_signal(near.at[stage], inc=1, device_id=peer, device_id_type=MESH)
 
     def met(stage):
-        for slot in range(len(meetings[stage])):
-            pl.semaphore_wait(near.at[stage, slot], 1)
+        pl.semaphore_wait(near.at[stage], len(meetings[stage]))
 
     for peer in peers:
         pl.semaphore_signal(barrier, inc=1, device_id=peer, device_id_type=MESH)
@@ -153,7 +153,13 @@
         for step in range(2):
             face_in[step, 1] = jnp.zeros(face_in.shape[2:], BF16)
 
-    far_first = at(lax.rem(y + half, ny), x, z) == 0
+    far = at(lax.rem(y + half, ny), x, z)
+    far_first = far == 0
+    far_last = far == last
+
+    @pl.when(far_last)
+    def _():
+        next_in[...] = jnp.zeros(next_in.shape, BF16)
 
     @pl.when(jnp.logical_not(far_first))
     def _():
@@ -182,6 +188,11 @@
     want = len(peers) + jnp.where(cells > 0, 1, 0) + jnp.where(cells < last, 1, 0)
     pl.semaphore_wait(barrier, want)
     meet(0)
+
+    @pl.when(cells < last)
+    def _():
+        pl.semaphore_signal(link, inc=1, device_id=(cells + 1, band), device_id_type=MESH)
+
     send_faces(0)
     loads[4].wait()
     t[96:EARLY, :] = mm(h[96:EARLY, :], u[0:NODES, :])
@@ -194,6 +205,11 @@
 
     wait_faces(0)
     met(0)
+
+    @pl.when(cells > 0)
+    def _():
+        pl.semaphore_wait(link, 1)
+
     meet(1)
     low1 = 0.5 * (low + face_in[0, 0, 0:SHARED, :].astype(F32))
     high1 = 0.5 * (high + face_in[0, 1, 0:SHARED, :].astype(F32))
@@ -210,15 +226,38 @@
     face_out[1, 0, 0:SHARED, :] = t[0:SHARED, :].astype(BF16)
     face_out[1, 1, 0:SHARED, :] = t[FAR:NODES, :].astype(BF16)
     send_faces(1)
+    prior = lax.rem(cells + last, last + 1)
+    prior_z, prior_x, prior_y = lax.rem(prior, nz), lax.rem(prior // nz, nx), prior // (nx * nz)
+
+    def next_copy(k):
+        if k < 2:
+            there = lax.rem(plane * ny + prior_y + half * (1 - 2 * k) + ring, ring)
+            peer = (at(lax.rem(there, ny), prior_x, prior_z), (there // ny) * 2 + core)
+            slot = plane
+        else:
+            peer = (at(lax.rem(prior_y + half, ny), prior_x, prior_z), (1 - plane) * 2 + 1 - core)
+            slot = 2
+        return pltpu.make_async_remote_copy(
+            face_out.at[1, 0], next_in.at[slot],
+            next_send.at[k], next_recv.at[k],
+            device_id=peer, device_id_type=MESH,
+        )
+
+    @pl.when(cells > 0)
+    def _():
+        for k in range(3):
+            next_copy(k).start()
+
     add_faces(96, EARLY)
 
     first = jnp.where(cells == 0, jnp.float32(1.0), jnp.float32(0.0))
     t[0:NODES, :] = t[0:NODES, :] - u[0:NODES, :].astype(F32)
     filt[0:NODES, :] = t[0:NODES, :].astype(BF16)
     filt[0:SHARED, :] = (t[0:SHARED, :] * first).astype(BF16)
+    filt[NODES:ROWS, :] = jnp.zeros((ROWS - NODES, WIDTH), BF16)
 
     def rows_of(part):
-        return (pl.ds(LOW, EARLY - LOW), pl.ds(EARLY, ROWS - EARLY), pl.ds(0, LOW))[part]
+        return (pl.ds(LOW, CUT - LOW), pl.ds(CUT, ROWS - CUT), pl.ds(0, LOW))[part]
 
     def f_copy(part, k):
         return pltpu.make_async_remote_copy(
@@ -227,44 +266,34 @@
             device_id=f_peers[k], device_id_type=MESH,
         )
 
-    for k in range(2):
-        f_copy(0, k).start()
+    for part in range(2):
+        for k in range(2):
+            f_copy(part, k).start()
 
     @pl.when(cells == 0)
     def _():
         for k in range(2):
             f_copy(2, k).start()
 
-    cross_copy = pltpu.make_async_remote_copy(
-        filt.at[rows_of(1)], far_twin.at[rows_of(1)],
-        w_send.at[1], w_recv.at[1], device_id=cross, device_id_type=MESH,
-    )
-
     wait_faces(1)
+    whole[0:EARLY, :] = filt[0:EARLY, :]
+    t[0:SHARED, :] += face_in[1, 0, 0:SHARED, :].astype(F32)
     t[FAR:NODES, :] += face_in[1, 1, 0:SHARED, :].astype(F32)
-    filt[EARLY:NODES, :] = t[EARLY:NODES, :].astype(BF16)
-    filt[NODES:ROWS, :] = jnp.zeros((ROWS - NODES, WIDTH), BF16)
-    for k in range(2):
-        f_copy(1, k).start()
-    cross_copy.start()
+    whole[EARLY:NODES, :] = t[EARLY:NODES, :].astype(BF16)
+    whole[NODES:ROWS, :] = jnp.zeros((ROWS - NODES, WIDTH), BF16)
     own_copy = pltpu.make_async_remote_copy(
-        filt, own_twin, w_send.at[3], w_recv.at[3], device_id=twin, device_id_type=MESH
+        whole, own_twin, w_send.at[3], w_recv.at[3], device_id=twin, device_id_type=MESH
     )
     own_copy.start()
     met(1)
     meet(2)
 
-    t[0:SHARED, :] += face_in[1, 0, 0:SHARED, :].astype(F32)
-    rows = lax.broadcasted_iota(jnp.int32, (NODES, NODES), 0).astype(F32)
-    place = jnp.where(rows == jnp.broadcast_to(order, (NODES, NODES)), 1.0, 0.0).astype(BF16)
-    full = t[0:NODES, :]
-    coarse = full.astype(BF16)
-    fine = (full - coarse.astype(F32)).astype(BF16)
-    out_ref[...] = mm(place, coarse) + mm(place, fine)
-
     def gram(part, left, one, two):
         for side, right in ((core, one), (1 - core, two)):
-            block = lax.dot_general(left, right, (((0,), (0,)), ((), ())), preferred_element_type=F32)
+            block = sum(
+                lax.dot_general(a, b, (((0,), (0,)), ((), ())), preferred_element_type=F32)
+                for a, b in zip(left, right)
+            )
             tiles = block.reshape(8, 16, WIDTH)
             gram_f[part, pl.ds(8 * side, 8)] = tiles
             gram_b[part, pl.ds(8 * side, 8)] = tiles.astype(BF16)
@@ -330,10 +359,6 @@
         for n in range(len(spans)):
             g_copy(part, n).start()
 
-    own_copy.wait_recv()
-    gram(0, filt[...], filt[...], own_twin[...])
-    scatter(0)
-
     def w_copy(part):
         return pltpu.make_async_remote_copy(
             fall.at[1 - plane, rows_of(part)], far_twin.at[rows_of(part)],
@@ -352,12 +377,45 @@
         w_copy(2).start()
         w_copy(2).wait_recv()
 
+    own_copy.wait_recv()
+    gram(0, [whole[...]], [whole[...]], [own_twin[...]])
+    scatter(0)
     for k in range(2):
         f_copy(1, k).wait_recv()
-    cross_copy.wait_recv()
-    w_copy(0).wait_recv()
-    gram(1, fall[plane], fall[1 - plane], far_twin[...])
+    w_copy(1).start()
+
+    @pl.when(jnp.logical_not(far_last))
+    def _():
+        for k in range(3):
+            next_copy(k).wait_recv()
+
+    def join(slot, rows):
+        late[slot] = rows
+        begin = FAR - EARLY
+        late[slot, begin:begin + SHARED, :] = (
+            rows[begin:begin + SHARED].astype(F32) + next_in[slot, 0:SHARED, :].astype(F32)
+        ).astype(BF16)
+
+    for k in range(2):
+        join(k, fall[k, EARLY:ROWS, :])
+    for part in range(2):
+        w_copy(part).wait_recv()
+    join(2, far_twin[EARLY:ROWS, :])
+    gram(
+        1,
+        [fall[plane, 0:EARLY, :], late[plane]],
+        [fall[1 - plane, 0:EARLY, :], late[1 - plane]],
+        [far_twin[0:EARLY, :], late[2]],
+    )
     scatter(1)
+
+    rows = lax.broadcasted_iota(jnp.int32, (NODES, NODES), 0).astype(F32)
+    place = jnp.where(rows == jnp.broadcast_to(order, (NODES, NODES)), 1.0, 0.0).astype(BF16)
+    full = t[0:NODES, :]
+    coarse = full.astype(BF16)
+    fine = (full - coarse.astype(F32)).astype(BF16)
+    out_ref[...] = mm(place, coarse) + mm(place, fine)
+
     met(2)
     exchange(0)
     exchange(1)
@@ -369,8 +427,8 @@
     done_faces(0)
     done_faces(1)
     own_copy.wait_send()
-    cross_copy.wait_send()
     w_copy(0).wait_send()
+    w_copy(1).wait_send()
 
     @pl.when(far_first)
     def _():
@@ -380,6 +438,11 @@
     def _():
         for k in range(2):
             f_copy(2, k).wait_send()
+
+    @pl.when(cells > 0)
+    def _():
+        for k in range(3):
+            next_copy(k).wait_send()
 
     for part in range(2):
         for k in range(2):
@@ -421,18 +484,22 @@
                 pltpu.VMEM((ROWS, WIDTH), F32),
                 pltpu.VMEM((ROWS, WIDTH), BF16),
                 pltpu.VMEM((ROWS, WIDTH), BF16),
+                pltpu.VMEM((ROWS, WIDTH), BF16),
                 pltpu.VMEM((2, ROWS, WIDTH), BF16),
                 pltpu.VMEM((ROWS, WIDTH), BF16),
                 pltpu.VMEM((ROWS, WIDTH), BF16),
+                pltpu.VMEM((3, 96, WIDTH), BF16),
                 pltpu.VMEM((2, 2, 96, WIDTH), BF16),
                 pltpu.VMEM((2, 2, 96, WIDTH), BF16),
+                pltpu.VMEM((3, 96, WIDTH), BF16),
                 pltpu.VMEM((2, 16, 16, WIDTH), F32),
                 pltpu.VMEM((2, 16, 16, WIDTH), BF16),
                 pltpu.VMEM((2, nx * ny - 1, 16, WIDTH), BF16),
                 pltpu.VMEM((2, nz, 16, WIDTH), BF16),
                 dma((5,)),
                 dma((2, 2)), dma((2, 2)),
-                pltpu.SemaphoreType.REGULAR((3, 5)),
+                pltpu.SemaphoreType.REGULAR((3,)), pltpu.SemaphoreType.REGULAR,
+                dma((3,)), dma((3,)),
                 dma((3, 2)), dma((3, 2)), dma((4,)), dma((4,)),
                 dma((2,)), dma((2,)), dma((2,)), dma((2,)), dma((2,)), dma((2,)),
             ],

time: 48.8 us -> 50.4 us (1.033)
  Pallas kernels: 48 us -> 49.6 us
    pallas_call x1, Pallas kernels: 47.2 us -> 48.8 us  [body(): pl.pallas_call(lambda *refs: kernel(sizes, *refs), out_shape=(jax.ShapeDt...]
where the time goes in v5:
time: 50.4 us; the launch traced here: 50.3 us
  Pallas kernels  49.6 us (98%)
  between operations  0.64 us (1%)
    pallas_call x1, Pallas kernels, body(): pl.pallas_call(lambda *refs: kernel(sizes, *refs), out_shape=(jax.ShapeDt...  48.8 us

profile of v5, /device:TPU:1, one launch (start us, length us, event | category | flops | bytes accessed | tf_op | source)
XLA Modules:
  0.0 50.3 jit_solution(14953536979825323696)
XLA Ops:
  0.6 48.8 %shard_map.50 = (f32[729,128]{1,0:T(8,128)S(1)}, bf16[2,16,16,128]{3,2,1,0:T(8,128)(2,1)S(1)}) custom-call(bf16[729,128]{1,0:T(8,128)(2,1)} %refs_0_.1, bf16[1,729,729]{2,1,0:T(8,128)(2,1)} %refs_1_.1, s32[1,729]{1,0:T(1,128)} %refs_2_.1), custom_call_target="tpu_custom_call" | custom-call | tf_op jit(solution)/shard_map/pallas_call | solution.py:471
  49.4 0.8 %shard_map.51 = (f32[729,128]{1,0:T(8,128)}, f32[512,128]{1,0:T(8,128)}) custom-call(f32[729,128]{1,0:T(8,128)S(1)} %get-tuple-element.4.filtered, bf16[4,128,128]{2,1,0:T(8,128)(2,1)S(1)} %bitcast.1), custom_call_target="tpu_custom_call" | custom-call | tf_op jit(solution)/shard_map/pallas_call | solution.py:510

commit v6 on v4

--- a/solution.py
+++ b/solution.py
@@ -25,9 +25,9 @@
     sizes,
     v_hbm, h_hbm, conn_hbm,
     out_ref, res,
-    v, h, conn, u, t, y1, filt, fall, own_twin, far_twin, face_out, face_in,
+    v, h, conn, u, t, y1, filt, fall, own_twin, far_twin, face_out, face_in, relay,
     gram_f, gram_b, rs_in, rz,
-    in_sem, face_send, face_recv, near, f_send, f_recv, w_send, w_recv,
+    in_sem, face_send, face_recv, relay_sem, near, f_send, f_recv, w_send, w_recv,
     s_send, s_recv, z_send, z_recv, g_send, g_recv,
 ):
     ny, nx, nz = sizes
@@ -90,12 +90,11 @@
     )
 
     def meet(stage):
-        for slot, peer in enumerate(meetings[stage]):
-            pl.semaphore_signal(near.at[stage, slot], inc=1, device_id=peer, device_id_type=MESH)
+        for peer in meetings[stage]:
+            pl.semaphore_signal(near.at[stage], inc=1, device_id=peer, device_id_type=MESH)
 
     def met(stage):
-        for slot in range(len(meetings[stage])):
-            pl.semaphore_wait(near.at[stage, slot], 1)
+        pl.semaphore_wait(near.at[stage], len(meetings[stage]))
 
     for peer in peers:
         pl.semaphore_signal(barrier, inc=1, device_id=peer, device_id_type=MESH)
@@ -104,9 +103,30 @@
     def _():
         pl.semaphore_signal(barrier, inc=1, device_id=(cells - 1, band), device_id_type=MESH)
 
-    @pl.when(cells < last)
+    block = nx * nz
+    is_after = jnp.logical_and(cells > 0, lax.rem(cells, block) == 0)
+    is_before = jnp.logical_and(cells < last, lax.rem(cells, block) == block - 1)
+    is_relay = jnp.logical_and(cells < last - nz, lax.rem(cells, block) == block - nz)
+
+    @pl.when(jnp.logical_and(cells < last, jnp.logical_not(is_before)))
     def _():
         pl.semaphore_signal(barrier, inc=1, device_id=(cells + 1, band), device_id_type=MESH)
+
+    @pl.when(is_relay)
+    def _():
+        pl.semaphore_signal(barrier, inc=1, device_id=(cells + nz, band), device_id_type=MESH)
+
+    def to_relay():
+        return pltpu.make_async_remote_copy(
+            face_out.at[0, 0], relay, relay_sem.at[0], relay_sem.at[1],
+            device_id=(cells - nz, band), device_id_type=MESH,
+        )
+
+    def from_relay():
+        return pltpu.make_async_remote_copy(
+            relay, face_in.at[0, 1], relay_sem.at[2], face_recv.at[0, 1],
+            device_id=(cells + nz - 1, band), device_id_type=MESH,
+        )
 
     def face_copy(step, side):
         peer = (cells - 1 + 2 * side, band)
@@ -182,7 +202,23 @@
     want = len(peers) + jnp.where(cells > 0, 1, 0) + jnp.where(cells < last, 1, 0)
     pl.semaphore_wait(barrier, want)
     meet(0)
-    send_faces(0)
+    @pl.when(jnp.logical_and(cells > 0, jnp.logical_not(is_after)))
+    def _():
+        face_copy(0, 0).start()
+
+    @pl.when(is_after)
+    def _():
+        to_relay().start()
+
+    @pl.when(cells < last)
+    def _():
+        face_copy(0, 1).start()
+
+    @pl.when(is_relay)
+    def _():
+        to_relay().wait_recv()
+        from_relay().start()
+
     loads[4].wait()
     t[96:EARLY, :] = mm(h[96:EARLY, :], u[0:NODES, :])
     y1[0:NODES, :] = (0.5 * t[0:NODES, :]).astype(BF16)
@@ -366,7 +402,22 @@
     for part in range(2):
         g_all(part).wait_recv()
 
-    done_faces(0)
+    @pl.when(jnp.logical_and(cells > 0, jnp.logical_not(is_after)))
+    def _():
+        face_copy(0, 0).wait_send()
+
+    @pl.when(is_after)
+    def _():
+        to_relay().wait_send()
+
+    @pl.when(is_relay)
+    def _():
+        from_relay().wait_send()
+
+    @pl.when(cells < last)
+    def _():
+        face_copy(0, 1).wait_send()
+
     done_faces(1)
     own_copy.wait_send()
     cross_copy.wait_send()
@@ -426,13 +477,15 @@
                 pltpu.VMEM((ROWS, WIDTH), BF16),
                 pltpu.VMEM((2, 2, 96, WIDTH), BF16),
                 pltpu.VMEM((2, 2, 96, WIDTH), BF16),
+                pltpu.VMEM((96, WIDTH), BF16),
                 pltpu.VMEM((2, 16, 16, WIDTH), F32),
                 pltpu.VMEM((2, 16, 16, WIDTH), BF16),
                 pltpu.VMEM((2, nx * ny - 1, 16, WIDTH), BF16),
                 pltpu.VMEM((2, nz, 16, WIDTH), BF16),
                 dma((5,)),
                 dma((2, 2)), dma((2, 2)),
-                pltpu.SemaphoreType.REGULAR((3, 5)),
+                dma((3,)),
+                pltpu.SemaphoreType.REGULAR((3,)),
                 dma((3, 2)), dma((3, 2)), dma((4,)), dma((4,)),
                 dma((2,)), dma((2,)), dma((2,)), dma((2,)), dma((2,)), dma((2,)),
             ],

time: 48.8 us -> 47.3 us (0.969)
  Pallas kernels: 48 us -> 46.5 us
    pallas_call x1, Pallas kernels: 47.2 us -> 45.6 us  [body(): pl.pallas_call(lambda *refs: kernel(sizes, *refs), out_shape=(jax.ShapeDt...]
where the time goes in v6:
time: 47.3 us; the launch traced here: 47.1 us
  Pallas kernels  46.5 us (98%)
  between operations  0.64 us (1%)
    pallas_call x1, Pallas kernels, body(): pl.pallas_call(lambda *refs: kernel(sizes, *refs), out_shape=(jax.ShapeDt...  45.6 us

profile of v6, /device:TPU:1, one launch (start us, length us, event | category | flops | bytes accessed | tf_op | source)
XLA Modules:
  0.0 47.1 jit_solution(7372287898609082710)
XLA Ops:
  0.6 45.6 %shard_map.50 = (f32[729,128]{1,0:T(8,128)S(1)}, bf16[2,16,16,128]{3,2,1,0:T(8,128)(2,1)S(1)}) custom-call(bf16[729,128]{1,0:T(8,128)(2,1)} %refs_0_.1, bf16[1,729,729]{2,1,0:T(8,128)(2,1)} %refs_1_.1, s32[1,729]{1,0:T(1,128)} %refs_2_.1), custom_call_target="tpu_custom_call" | custom-call | tf_op jit(solution)/shard_map/pallas_call | solution.py:459
  46.3 0.8 %shard_map.51 = (f32[729,128]{1,0:T(8,128)}, f32[512,128]{1,0:T(8,128)}) custom-call(f32[729,128]{1,0:T(8,128)S(1)} %get-tuple-element.4.filtered, bf16[4,128,128]{2,1,0:T(8,128)(2,1)S(1)} %bitcast.1), custom_call_target="tpu_custom_call" | custom-call | tf_op jit(solution)/shard_map/pallas_call | solution.py:496

commit v7 on v6

--- a/solution.py
+++ b/solution.py
@@ -259,9 +259,16 @@
     def f_copy(part, k):
         return pltpu.make_async_remote_copy(
             filt.at[rows_of(part)], fall.at[plane, rows_of(part)],
-            f_send.at[part, k], f_recv.at[part, k],
+            f_send.at[part, k], f_recv.at[part, plane],
             device_id=f_peers[k], device_id_type=MESH,
         )
+
+    def f_wait(part, source):
+        pltpu.make_async_remote_copy(
+            filt.at[rows_of(part)], fall.at[source, rows_of(part)],
+            f_send.at[part, 0], f_recv.at[part, source],
+            device_id=f_peers[0], device_id_type=MESH,
+        ).wait_recv()
 
     for k in range(2):
         f_copy(0, k).start()
@@ -290,13 +297,6 @@
     met(1)
     meet(2)
 
-    t[0:SHARED, :] += face_in[1, 0, 0:SHARED, :].astype(F32)
-    rows = lax.broadcasted_iota(jnp.int32, (NODES, NODES), 0).astype(F32)
-    place = jnp.where(rows == jnp.broadcast_to(order, (NODES, NODES)), 1.0, 0.0).astype(BF16)
-    full = t[0:NODES, :]
-    coarse = full.astype(BF16)
-    fine = (full - coarse.astype(F32)).astype(BF16)
-    out_ref[...] = mm(place, coarse) + mm(place, fine)
 
     def gram(part, left, one, two):
         for side, right in ((core, one), (1 - core, two)):
@@ -377,23 +377,30 @@
             device_id=twin, device_id_type=MESH,
         )
 
-    for k in range(2):
-        f_copy(0, k).wait_recv()
+    f_wait(0, 1 - plane)
     w_copy(0).start()
+    f_wait(0, plane)
 
     @pl.when(far_first)
     def _():
         for k in range(2):
-            f_copy(2, k).wait_recv()
+            f_wait(2, k)
         w_copy(2).start()
         w_copy(2).wait_recv()
 
     for k in range(2):
-        f_copy(1, k).wait_recv()
+        f_wait(1, k)
     cross_copy.wait_recv()
     w_copy(0).wait_recv()
     gram(1, fall[plane], fall[1 - plane], far_twin[...])
     scatter(1)
+    t[0:SHARED, :] += face_in[1, 0, 0:SHARED, :].astype(F32)
+    rows = lax.broadcasted_iota(jnp.int32, (NODES, NODES), 0).astype(F32)
+    place = jnp.where(rows == jnp.broadcast_to(order, (NODES, NODES)), 1.0, 0.0).astype(BF16)
+    full = t[0:NODES, :]
+    coarse = full.astype(BF16)
+    fine = (full - coarse.astype(F32)).astype(BF16)
+    out_ref[...] = mm(place, coarse) + mm(place, fine)
     met(2)
     exchange(0)
     exchange(1)

time: 47.3 us -> 47.1 us (level)
  no operation moved by 1% of the time
where the time goes in v7:
time: 47.1 us; the launch traced here: 46.9 us
  Pallas kernels  46.3 us (98%)
  between operations  0.64 us (1%)
    pallas_call x1, Pallas kernels, body(): pl.pallas_call(lambda *refs: kernel(sizes, *refs), out_shape=(jax.ShapeDt...  45.5 us

profile of v7, /device:TPU:1, one launch (start us, length us, event | category | flops | bytes accessed | tf_op | source)
XLA Modules:
  0.0 46.9 jit_solution(5682398183860658440)
XLA Ops:
  0.6 45.5 %shard_map.50 = (f32[729,128]{1,0:T(8,128)S(1)}, bf16[2,16,16,128]{3,2,1,0:T(8,128)(2,1)S(1)}) custom-call(bf16[729,128]{1,0:T(8,128)(2,1)} %refs_0_.1, bf16[1,729,729]{2,1,0:T(8,128)(2,1)} %refs_1_.1, s32[1,729]{1,0:T(1,128)} %refs_2_.1), custom_call_target="tpu_custom_call" | custom-call | tf_op jit(solution)/shard_map/pallas_call | solution.py:466
  46.1 0.8 %shard_map.51 = (f32[729,128]{1,0:T(8,128)}, f32[512,128]{1,0:T(8,128)}) custom-call(f32[729,128]{1,0:T(8,128)S(1)} %get-tuple-element.4.filtered, bf16[4,128,128]{2,1,0:T(8,128)(2,1)S(1)} %bitcast.1), custom_call_target="tpu_custom_call" | custom-call | tf_op jit(solution)/shard_map/pallas_call | solution.py:503

commit v8 on v7

--- a/solution.py
+++ b/solution.py
@@ -77,9 +77,6 @@
         ),
         pltpu.make_async_copy(h_hbm.at[0, pl.ds(96, EARLY - 96)], h.at[pl.ds(96, EARLY - 96)], in_sem.at[4]),
     ]
-    for load in loads:
-        load.start()
-
     barrier = pltpu.get_barrier_semaphore()
     cross = (at(lax.rem(y + half, ny), x, z), (1 - plane) * 2 + 1 - core)
     peers = f_peers + [cross, twin, xy_peer(0, 1), x_peer(1), x_peer(-1), z_peer(1), z_peer(-1)]
@@ -127,6 +124,9 @@
             relay, face_in.at[0, 1], relay_sem.at[2], face_recv.at[0, 1],
             device_id=(cells + nz - 1, band), device_id_type=MESH,
         )
+
+    for load in loads:
+        load.start()
 
     def face_copy(step, side):
         peer = (cells - 1 + 2 * side, band)
@@ -201,18 +201,19 @@
     face_out[0, 1, 0:SHARED, :] = t[FAR:NODES, :].astype(BF16)
     want = len(peers) + jnp.where(cells > 0, 1, 0) + jnp.where(cells < last, 1, 0)
     pl.semaphore_wait(barrier, want)
+    @pl.when(jnp.logical_and(cells > 0, jnp.logical_not(is_after)))
+    def _():
+        face_copy(0, 0).start()
+
+    @pl.when(is_after)
+    def _():
+        to_relay().start()
+
+    @pl.when(cells < last)
+    def _():
+        face_copy(0, 1).start()
+
     meet(0)
-    @pl.when(jnp.logical_and(cells > 0, jnp.logical_not(is_after)))
-    def _():
-        face_copy(0, 0).start()
-
-    @pl.when(is_after)
-    def _():
-        to_relay().start()
-
-    @pl.when(cells < last)
-    def _():
-        face_copy(0, 1).start()
 
     @pl.when(is_relay)
     def _():

time: 47.1 us -> 47.1 us (level)
  no operation moved by 1% of the time
where the time goes in v8:
time: 47.1 us; the launch traced here: 47 us
  Pallas kernels  46.3 us (98%)
  between operations  0.64 us (1%)
    pallas_call x1, Pallas kernels, body(): pl.pallas_call(lambda *refs: kernel(sizes, *refs), out_shape=(jax.ShapeDt...  45.5 us

profile of v8, /device:TPU:1, one launch (start us, length us, event | category | flops | bytes accessed | tf_op | source)
XLA Modules:
  0.0 47.0 jit_solution(11211083797974826687)
XLA Ops:
  0.6 45.5 %shard_map.50 = (f32[729,128]{1,0:T(8,128)S(1)}, bf16[2,16,16,128]{3,2,1,0:T(8,128)(2,1)S(1)}) custom-call(bf16[729,128]{1,0:T(8,128)(2,1)} %refs_0_.1, bf16[1,729,729]{2,1,0:T(8,128)(2,1)} %refs_1_.1, s32[1,729]{1,0:T(1,128)} %refs_2_.1), custom_call_target="tpu_custom_call" | custom-call | tf_op jit(solution)/shard_map/pallas_call | solution.py:467
  46.1 0.8 %shard_map.51 = (f32[729,128]{1,0:T(8,128)}, f32[512,128]{1,0:T(8,128)}) custom-call(f32[729,128]{1,0:T(8,128)S(1)} %get-tuple-element.4.filtered, bf16[4,128,128]{2,1,0:T(8,128)(2,1)S(1)} %bitcast.1), custom_call_target="tpu_custom_call" | custom-call | tf_op jit(solution)/shard_map/pallas_call | solution.py:504
